TPU v7x, 32 devices: a whole 2x2x4 slice. The times are simulated.
32 devices in a mesh: group: 2 (over y), gz: 4 (over z), gy: 2 (over x), gx: 2 (over core).
Axes of the slice: x: 2, y: 2, z: 4, core: 2. Of those that a mesh axis runs over, the one named last changes fastest.
Arguments:
- volume: bfloat16 [32, 32, 16, 512], P(None, ('group', 'gz'), 'gy', 'gx'), parts along dimension 1, may hold values from -6 to 6
- first_weight: bfloat16 [3, 3, 3, 32, 32], replicated, may hold values from -0.21875 to 0.21875
- second_weight: bfloat16 [3, 3, 3, 32, 32], replicated, may hold values from -0.21875 to 0.21875
- sample_index: int32 [8, 2, 2, 256], P(('group', 'gz'), 'gy', 'gx'), parts along dimension 0, may hold values from 0 to 8191
- segments: int32 [8, 2, 2, 256], P('group', 'gy', 'gx'), parts along dimension 0, may hold values from 0 to 63
- block_match: int32 [8, 4], P('group'), parts along dimension 0, may hold values from 0 to 1, as said below
Outputs:
- features: bfloat16 [32, 32, 16, 512], P(None, ('group', 'gz'), 'gy', 'gx'), parts along dimension 1
- row_loss: float32 [8, 2, 2, 256], P(('group', 'gz'), 'gy', 'gx'), parts along dimension 0
There are 2 independent parts, one for each index of `group`. A program takes and returns all parts, laid end to end along the dimension named above; an argument that names none is the same for every part. Nothing has to cross between parts.
Inputs may be any that keep to these rules, and one draw needn't show every extreme that they name: `sample_index`: the voxel of a row is z * 8 * 256 + y * 256 + x in its block's local coordinates. `block_match`: entry [a, a2] is 1 when block a contrasts against block a2; the diagonal is 1.
All inputs are finite; a program needn't handle non-finite values.
Results may differ from a plain program's by a relative error of at most 0.0034.
Values may be sent and summed in bfloat16 or wider, within the bound.
A program may use at most 128 MiB of HBM per device.

v0:
```python
import jax
import jax.numpy as jnp
from jax import lax
from jax.sharding import PartitionSpec as P

SOFTMAX_WARMTH = 0.25


def extended(shard, sides, width):
    for axis, dim in sides:
        count, length = (lax.axis_size(axis), shard.shape[dim])
        up = [(i, (i + 1) % count) for i in range(count - 1)]
        down = [(j, i) for i, j in up]
        last = lax.slice_in_dim(shard, length - width, length, axis=dim)
        leading = lax.slice_in_dim(shard, 0, width, axis=dim)
        before = lax.ppermute(last, axis, up)
        after = lax.ppermute(leading, axis, down)
        shard = jnp.concatenate([before, shard, after], axis=dim)
    return shard


def conv_valid(padded, weight):
    channels = padded.shape[0]
    out_z = padded.shape[1] - 2
    out_y = padded.shape[2] - 2
    out_x = padded.shape[3] - 2
    outputs = weight.shape[3]
    reduced_total = jnp.zeros((outputs, out_z * out_y * out_x), jnp.float32)
    for offset_z in range(3):
        plane = padded[:, offset_z : offset_z + out_z]
        stacked = jnp.stack(
            [
                plane[:, :, offset_y : offset_y + out_y, column_shift : column_shift + out_x]
                for offset_y in range(3)
                for column_shift in range(3)
            ],
            axis=0,
        )
        patches = stacked.reshape(9 * channels, out_z * out_y * out_x)
        kernel = jnp.transpose(weight[offset_z], (2, 0, 1, 3)).reshape(outputs, 9 * channels)
        reduced_total = reduced_total + jnp.dot(kernel, patches, preferred_element_type=jnp.float32)
    return reduced_total.reshape(outputs, out_z, out_y, out_x)


def pad_layer(activ_in):
    return extended(activ_in, (("gz", 1), ("gy", 2), ("gx", 3)), 1)


def shards(volume, first_weight, second_weight, sample_index, segments, block_match):
    channels, slab_depth, tile_height, tile_width = volume.shape
    hidden = jax.nn.relu(conv_valid(pad_layer(volume), first_weight)).astype(jnp.bfloat16)
    conv_out = conv_valid(pad_layer(hidden), second_weight)
    features = (conv_out + volume.astype(jnp.float32)).astype(jnp.bfloat16)
    flattened = features.reshape(channels, -1)
    picked = jnp.take(flattened, sample_index.reshape(-1), axis=1).astype(jnp.float32)
    embedding = (picked / jnp.sqrt(jnp.sum(picked * picked, axis=0) + 1.0)).astype(jnp.bfloat16)
    query_rows = embedding[None]
    own_block = lax.axis_index("gz")
    seg_all = segments.reshape(segments.shape[0], -1)
    home_segment_label = lax.dynamic_index_in_dim(seg_all, own_block, 0, keepdims=False)
    match_float = block_match.astype(jnp.float32)
    rows = embedding.shape[1]
    match_row = lax.dynamic_index_in_dim(match_float, own_block, 0, keepdims=False)
    similarity_logits = (
        jnp.einsum(
            "cr,kcs->rks",
            embedding,
            lax.all_gather(query_rows, "gz", axis=0, tiled=True),
            preferred_element_type=jnp.float32,
        )
        / SOFTMAX_WARMTH
    )
    same_seg = (home_segment_label[:, None, None] == seg_all[None]).astype(jnp.float32)
    exp_terms = jnp.exp(similarity_logits) * match_row[None, :, None]
    reduced_total = jnp.sum(exp_terms, axis=(1, 2))
    positive = jnp.sum(exp_terms * same_seg, axis=(1, 2))
    row_loss = (jnp.log(reduced_total) - jnp.log(positive)).reshape(1, 1, 1, rows)
    return (features, row_loss)


def solution(mesh):
    in_specs = (
        P(None, ("group", "gz"), "gy", "gx"),
        P(),
        P(),
        P(("group", "gz"), "gy", "gx", None),
        P("group", "gy", "gx", None),
        P("group", None),
    )
    out_specs = (P(None, ("group", "gz"), "gy", "gx"), P(("group", "gz"), "gy", "gx", None))
    return jax.shard_map(shards, mesh=mesh, in_specs=in_specs, out_specs=out_specs, check_vma=False)
```

profile of v0, /device:TPU:0, one launch (start us, length us, event | category | flops | bytes accessed | tf_op | source)
XLA Modules:
  0.0 274.9 jit_solution(13628984462543033317)
XLA Ops:
  1.6 4.9 %collective-permute-start = (bf16[32,1,8,256]{3,2,1,0:T(8,128)(2,1)S(1)}, bf16[32,1,8,256]{3,2,1,0:T(8,128)(2,1)S(1)}, u32[]{:S(2)}, u32[]{:S(2)}) collective-permute-start(bf16[32,1,8,256]{3,2,1,0:T(8,128)(2,1)S(1)} %get-tuple-element.74), channel_id=1, source_target_pairs={{0,4},{4,8},{8,12},{1,5},{5,9},{9,13},{2,6},{6,10},{10,14},{3,7},{... | collective-permute-start | bytes 393224 | tf_op jit(solution)/shard_map/ppermute | solution.py:16
  6.6 1.3 collective-permute-start.1
  8.9 1.6 slice_bitcast_fusion
  13.5 3.5 %copy.224 = bf16[32,6,8,256]{0,1,3,2:T(8,128)(2,1)} copy(bf16[32,6,8,256]{3,2,1,0:T(8,128)(2,1)S(1)} %constant_dynamic-update-slice_fusion) | data formatting | bytes 1572864 | tf_op jit(solution)/shard_map/concatenate | solution.py:18
  17.0 2.4 fusion.111
  19.4 3.4 %collective-permute-start.2 = (bf16[32,6,1,256]{0,1,3,2:T(8,128)(2,1)}, bf16[32,6,1,256]{0,1,3,2:T(8,128)(2,1)S(1)}, u32[]{:S(2)}, u32[]{:S(2)}) collective-permute-start(bf16[32,6,1,256]{0,1,3,2:T(8,128)(2,1)} %get-tuple-element.10), channel_id=1, source_target_pairs={{0,2},{1,3},{4,6},{5,7},{8,10},{9,11},{12,14},{13,15},{16,18},{17,... | collective-permute-start | bytes 294920 | tf_op jit(solution)/shard_map/ppermute | solution.py:16
  22.8 1.3 collective-permute-start.3
  25.4 7.4 %collective-permute-done.2 = bf16[32,6,1,256]{0,1,3,2:T(8,128)(2,1)S(1)} collective-permute-done((bf16[32,6,1,256]{0,1,3,2:T(8,128)(2,1)}, bf16[32,6,1,256]{0,1,3,2:T(8,128)(2,1)S(1)}, u32[]{:S(2)}, u32[]{:S(2)}) %collective-permute-start.2) | collective-permute-done | bytes 98336 | tf_op jit(solution)/shard_map/ppermute | solution.py:16
  32.8 4.0 %collective-permute-done.3 = bf16[32,6,1,256]{0,1,3,2:T(8,128)(2,1)S(1)} collective-permute-done((bf16[32,6,1,256]{0,1,3,2:T(8,128)(2,1)}, bf16[32,6,1,256]{0,1,3,2:T(8,128)(2,1)S(1)}, u32[]{:S(2)}, u32[]{:S(2)}) %collective-permute-start.3) | collective-permute-done | bytes 98336 | tf_op jit(solution)/shard_map/ppermute | solution.py:17
  36.8 3.8 %pad_maximum_fusion = bf16[32,6,10,256]{0,1,3,2:T(8,128)(2,1)S(1)} fusion(bf16[32,6,1,256]{0,1,3,2:T(8,128)(2,1)S(1)} %collective-permute-done.3, bf16[32,6,8,256]{0,1,3,2:T(8,128)(2,1)} %copy.224, bf16[32,6,1,256]{0,1,3,2:T(8,128)(2,1)S(1)} %collective-permute-done.2), kind=kLoop, calls=%fused_computation.7 | loop fusion | flops 983040 | bytes 1966080 | tf_op jit(solution)/shard_map/concatenate | solution.py:18
  40.7 2.3 copy-done
  44.3 1.6 collective-permute-start.5
  46.5 1.7 fusion.93
  48.2 4.5 %copy.228 = bf16[32,6,10,256]{3,0,2,1:T(8,128)(2,1)S(1)} copy(bf16[32,6,10,256]{0,1,3,2:T(8,128)(2,1)} %copy-done) | data formatting | bytes 1966080 | tf_op jit(solution)/shard_map/concatenate | solution.py:18
  53.2 3.6 %fusion.94 = (bf16[1,32,4,8,256]{4,1,3,2,0:T(8,128)(2,1)}, bf16[1,32,4,8,256]{4,1,3,2,0:T(8,128)(2,1)S(1)}, bf16[1,32,4,8,256]{4,1,3,2,0:T(8,128)(2,1)}, bf16[1,...) fusion(bf16[32,6,10,256]{3,0,2,1:T(8,128)(2,1)S(1)} %copy.228, ...), kind=kLoop, calls=%fused_computation.193 | loop fusion | flops 9437184 | bytes 5705472 | tf_op jit(solution)/shard_map/stack | solution.py:31
  59.1 5.1 %fusion.92 = (bf16[1,32,4,8,256]{4,1,3,2,0:T(8,128)(2,1)S(1)}, bf16[1,32,4,8,256]{4,1,3,2,0:T(8,128)(2,1)S(1)}, bf16[1,32,4,8,256]{4,1,3,2,0:T(8,128)(2,1)S(1)},...) fusion(bf16[32,6,10,1]{3,0,2,1:T(8,128)(2,1)} %copy.232, ...), kind=kLoop, calls=%fused_computation.189 | loop fusion | flops 9437184 | bytes 5705472 | tf_op jit(solution)/shard_map/stack | solution.py:31
  66.4 2.2 copy_dynamic-update-slice_fusion.46
  80.8 1.6 copy_dynamic-update-slice_fusion.26
  84.5 8.4 %reshape.195 = bf16[288,8192]{1,0:T(8,128)(2,1)} reshape(bf16[9,32,4,8,256]{4,3,2,1,0:T(8,128)(2,1)} %copy_dynamic-update-slice_fusion.24) | data formatting | bytes 9437184 | tf_op jit(solution)/shard_map/reshape | solution.py:39
  92.9 2.1 copy_dynamic-update-slice_fusion.33
  96.1 8.8 %reshape.193 = bf16[288,8192]{1,0:T(8,128)(2,1)} reshape(bf16[9,32,4,8,256]{4,3,2,1,0:T(8,128)(2,1)} %copy_dynamic-update-slice_fusion.32) | data formatting | bytes 9437184 | tf_op jit(solution)/shard_map/reshape | solution.py:39
  109.3 8.3 %reshape.191 = bf16[288,8192]{1,0:T(8,128)(2,1)} reshape(bf16[9,32,4,8,256]{4,3,2,1,0:T(8,128)(2,1)} %copy_dynamic-update-slice_fusion.40) | data formatting | bytes 9437184 | tf_op jit(solution)/shard_map/reshape | solution.py:39
  117.6 3.5 %fusion.114 = f32[8192,32]{0,1:T(8,128)S(1)} fusion(bf16[32,288]{1,0:T(8,128)(2,1)S(1)} %reshape.192, bf16[288,8192]{1,0:T(8,128)(2,1)} %reshape.191), kind=kOutput, calls=%fused_computation.291 | convolution fusion | flops 150994944 | bytes 5785600 | tf_op jit(solution)/shard_map/dot_general | solution.py:41
  121.1 3.4 %convolution_add_fusion.3 = f32[8192,32]{0,1:T(8,128)S(1)} fusion(f32[8192,32]{0,1:T(8,128)S(1)} %fusion.114, bf16[32,288]{1,0:T(8,128)(2,1)S(1)} %reshape.194, bf16[288,8192]{1,0:T(8,128)(2,1)} %reshape.193), kind=kOutput, calls=%fused_computation.5 | convolution fusion | flops 151257088 | bytes 6834176 | tf_op jit(solution)/shard_map/dot_general | solution.py:41
  125.7 4.3 %collective-permute-start.6 = (bf16[32,1,8,256]{3,2,1,0:T(8,128)(2,1)S(1)}, bf16[32,1,8,256]{3,2,1,0:T(8,128)(2,1)S(1)}, u32[]{:S(2)}, u32[]{:S(2)}) collective-permute-start(bf16[32,1,8,256]{3,2,1,0:T(8,128)(2,1)S(1)} %get-tuple-element.69), channel_id=1, source_target_pairs={{0,4},{4,8},{8,12},{1,5},{5,9},{9,13},{2,6},{6,10},{10,14},{3,7},{... | collective-permute-start | bytes 393224 | tf_op jit(solution)/shard_map/ppermute | solution.py:16
  133.8 6.7 %collective-permute-done.7 = bf16[32,1,8,256]{3,2,1,0:T(8,128)(2,1)S(1)} collective-permute-done((bf16[32,1,8,256]{3,2,1,0:T(8,128)(2,1)S(1)}, bf16[32,1,8,256]{3,2,1,0:T(8,128)(2,1)S(1)}, u32[]{:S(2)}, u32[]{:S(2)}) %collective-permute-start.7) | collective-permute-done | bytes 131104 | tf_op jit(solution)/shard_map/ppermute | solution.py:17
  140.5 3.5 %copy.262 = bf16[32,6,8,256]{0,1,3,2:T(8,128)(2,1)} copy(bf16[32,6,8,256]{3,2,1,0:T(8,128)(2,1)S(1)} %constant_dynamic-update-slice_fusion.3) | data formatting | bytes 1572864 | tf_op jit(solution)/shard_map/concatenate | solution.py:18
  144.0 1.4 fusion.110
  145.4 1.6 collective-permute-start.8
  149.1 9.1 %collective-permute-done.8 = bf16[32,6,1,256]{0,1,3,2:T(8,128)(2,1)S(1)} collective-permute-done((bf16[32,6,1,256]{0,1,3,2:T(8,128)(2,1)S(1)}, bf16[32,6,1,256]{0,1,3,2:T(8,128)(2,1)S(1)}, u32[]{:S(2)}, u32[]{:S(2)}) %collective-permute-start.8) | collective-permute-done | bytes 98336 | tf_op jit(solution)/shard_map/ppermute | solution.py:16
  158.3 4.1 %collective-permute-done.9 = bf16[32,6,1,256]{0,1,3,2:T(8,128)(2,1)S(1)} collective-permute-done((bf16[32,6,1,256]{0,1,3,2:T(8,128)(2,1)S(1)}, bf16[32,6,1,256]{0,1,3,2:T(8,128)(2,1)S(1)}, u32[]{:S(2)}, u32[]{:S(2)}) %collective-permute-start.9) | collective-permute-done | bytes 98336 | tf_op jit(solution)/shard_map/ppermute | solution.py:17
  162.4 4.0 %pad_maximum_fusion.1 = bf16[32,6,10,256]{0,1,3,2:T(8,128)(2,1)S(1)} fusion(bf16[32,6,1,256]{0,1,3,2:T(8,128)(2,1)S(1)} %collective-permute-done.9, bf16[32,6,8,256]{0,1,3,2:T(8,128)(2,1)} %copy.262, bf16[32,6,1,256]{0,1,3,2:T(8,128)(2,1)S(1)} %collective-permute-done.8), kind=kLoop, calls=%fused_computation.8 | loop fusion | flops 983040 | bytes 1966080 | tf_op jit(solution)/shard_map/concatenate | solution.py:18
  166.5 2.3 copy-done.1
  173.6 1.7 fusion.85
  175.4 4.7 %copy.266 = bf16[32,6,10,256]{3,0,2,1:T(8,128)(2,1)S(1)} copy(bf16[32,6,10,256]{0,1,3,2:T(8,128)(2,1)} %copy-done.1) | data formatting | bytes 1966080 | tf_op jit(solution)/shard_map/concatenate | solution.py:18
  180.5 3.7 %fusion.86 = (bf16[1,32,4,8,256]{4,1,3,2,0:T(8,128)(2,1)}, bf16[1,32,4,8,256]{4,1,3,2,0:T(8,128)(2,1)S(1)}, bf16[1,32,4,8,256]{4,1,3,2,0:T(8,128)(2,1)}, bf16[1,...) fusion(bf16[32,6,10,256]{3,0,2,1:T(8,128)(2,1)S(1)} %copy.266, ...), kind=kLoop, calls=%fused_computation.179 | loop fusion | flops 9437184 | bytes 5705472 | tf_op jit(solution)/shard_map/stack | solution.py:31
  186.5 5.4 %fusion.84 = (bf16[1,32,4,8,256]{4,1,3,2,0:T(8,128)(2,1)S(1)}, bf16[1,32,4,8,256]{4,1,3,2,0:T(8,128)(2,1)S(1)}, bf16[1,32,4,8,256]{4,1,3,2,0:T(8,128)(2,1)}, bf1...) fusion(bf16[32,6,10,1]{3,0,2,1:T(8,128)(2,1)} %copy.270, ...), kind=kLoop, calls=%fused_computation.175 | loop fusion | flops 9437184 | bytes 5705472 | tf_op jit(solution)/shard_map/stack | solution.py:31
  193.1 2.2 copy_dynamic-update-slice_fusion.22
  206.2 8.3 %reshape.201 = bf16[288,8192]{1,0:T(8,128)(2,1)} reshape(bf16[9,32,4,8,256]{4,3,2,1,0:T(8,128)(2,1)} %copy_dynamic-update-slice_fusion) | data formatting | bytes 9437184 | tf_op jit(solution)/shard_map/reshape | solution.py:39
  214.5 2.3 copy_dynamic-update-slice_fusion.15
  216.8 2.1 copy_dynamic-update-slice_fusion.14
  218.9 2.1 copy_dynamic-update-slice_fusion.13
  221.1 2.1 copy_dynamic-update-slice_fusion.12
  228.4 8.5 %reshape.199 = bf16[288,8192]{1,0:T(8,128)(2,1)} reshape(bf16[9,32,4,8,256]{4,3,2,1,0:T(8,128)(2,1)} %copy_dynamic-update-slice_fusion.8) | data formatting | bytes 9437184 | tf_op jit(solution)/shard_map/reshape | solution.py:39
  241.3 8.3 %reshape.197 = bf16[288,8192]{1,0:T(8,128)(2,1)} reshape(bf16[9,32,4,8,256]{4,3,2,1,0:T(8,128)(2,1)} %copy_dynamic-update-slice_fusion.16) | data formatting | bytes 9437184 | tf_op jit(solution)/shard_map/reshape | solution.py:39
  249.6 3.5 %fusion.115 = f32[8192,32]{0,1:T(8,128)S(1)} fusion(bf16[32,288]{1,0:T(8,128)(2,1)S(1)} %copy-done.32, bf16[288,8192]{1,0:T(8,128)(2,1)} %reshape.197), kind=kOutput, calls=%fused_computation.292 | convolution fusion | flops 150994944 | bytes 5785600 | tf_op jit(solution)/shard_map/dot_general | solution.py:41
  253.1 3.4 %convolution_add_fusion.1 = f32[8192,32]{0,1:T(8,128)S(1)} fusion(f32[8192,32]{0,1:T(8,128)S(1)} %fusion.115, bf16[32,288]{1,0:T(8,128)(2,1)S(1)} %copy-done.33, bf16[288,8192]{1,0:T(8,128)(2,1)} %reshape.199), kind=kOutput, calls=%fused_computation.2 | convolution fusion | flops 151257088 | bytes 6834176 | tf_op jit(solution)/shard_map/dot_general | solution.py:41
  260.2 13.4 %all_gather.3 = bf16[4,32,256]{2,1,0:T(8,128)(2,1)S(1)} all-gather(bf16[1,32,256]{2,1,0:T(8,128)(2,1)S(1)} %divide_convert_fusion), channel_id=1, replica_groups=mesh['group'=2,'gz'=4,'gy'=2,'gx'=2] {'gz'}, dimensions={0}, use_global_device_ids=true | all-gather | bytes 81920 | tf_op jit(solution)/shard_map/all_gather | solution.py:68
  (195 shorter events, 73.7 us)
Async XLA Ops:
  1.6 9.6 %collective-permute-start = (bf16[32,1,8,256]{3,2,1,0:T(8,128)(2,1)S(1)}, bf16[32,1,8,256]{3,2,1,0:T(8,128)(2,1)S(1)}, u32[]{:S(2)}, u32[]{:S(2)}) collective-permute-start(bf16[32,1,8,256]{3,2,1,0:T(8,128)(2,1)S(1)} %get-tuple-element.74), channel_id=1, source_target_pairs={{0,4},{4,8},{8,12},{1,5},{5,9},{9,13},{2,6},{6,10},{10,14},{3,7},{... | collective-permute-start | bytes 393224 | tf_op jit(solution)/shard_map/ppermute | solution.py:16
  6.6 17.5 %copy-start.37 = (s32[1,1,1,256]{3,2,1,0:T(1,128)S(1)}, s32[1,1,1,256]{3,2,1,0:T(1,128)}, u32[]{:S(2)}) copy-start(s32[1,1,1,256]{3,2,1,0:T(1,128)} %param.9) | copy-start | bytes 3076
  6.6 6.9 %collective-permute-start.1 = (bf16[32,1,8,256]{3,2,1,0:T(8,128)(2,1)S(1)}, bf16[32,1,8,256]{3,2,1,0:T(8,128)(2,1)S(1)}, u32[]{:S(2)}, u32[]{:S(2)}) collective-permute-start(bf16[32,1,8,256]{3,2,1,0:T(8,128)(2,1)S(1)} %get-tuple-element.73), channel_id=1, source_target_pairs={{4,0},{8,4},{12,8},{5,1},{9,5},{13,9},{6,2},{10,6},{14,10},{7,3},{... | collective-permute-start | bytes 393224 | tf_op jit(solution)/shard_map/ppermute | solution.py:17
  19.4 13.5 %collective-permute-start.2 = (bf16[32,6,1,256]{0,1,3,2:T(8,128)(2,1)}, bf16[32,6,1,256]{0,1,3,2:T(8,128)(2,1)S(1)}, u32[]{:S(2)}, u32[]{:S(2)}) collective-permute-start(bf16[32,6,1,256]{0,1,3,2:T(8,128)(2,1)} %get-tuple-element.10), channel_id=1, source_target_pairs={{0,2},{1,3},{4,6},{5,7},{8,10},{9,11},{12,14},{13,15},{16,18},{17,... | collective-permute-start | bytes 294920 | tf_op jit(solution)/shard_map/ppermute | solution.py:16
  22.8 14.1 %collective-permute-start.3 = (bf16[32,6,1,256]{0,1,3,2:T(8,128)(2,1)}, bf16[32,6,1,256]{0,1,3,2:T(8,128)(2,1)S(1)}, u32[]{:S(2)}, u32[]{:S(2)}) collective-permute-start(bf16[32,6,1,256]{0,1,3,2:T(8,128)(2,1)} %get-tuple-element.11), channel_id=1, source_target_pairs={{2,0},{3,1},{6,4},{7,5},{10,8},{11,9},{14,12},{15,13},{18,16},{19,... | collective-permute-start | bytes 294920 | tf_op jit(solution)/shard_map/ppermute | solution.py:17
  43.0 9.7 %collective-permute-start.4 = (bf16[32,6,10,1]{0,1,3,2:T(8,128)(2,1)S(1)}, bf16[32,6,10,1]{0,1,3,2:T(8,128)(2,1)S(1)}, u32[]{:S(2)}, u32[]{:S(2)}) collective-permute-start(bf16[32,6,10,1]{0,1,3,2:T(8,128)(2,1)S(1)} %get-tuple-element.7), channel_id=1, source_target_pairs={{0,1},{2,3},{4,5},{6,7},{8,9},{10,11},{12,13},{14,15},{16,17},{18,... | collective-permute-start | bytes 11528 | tf_op jit(solution)/shard_map/ppermute | solution.py:16
  44.3 13.5 %collective-permute-start.5 = (bf16[32,6,10,1]{0,1,3,2:T(8,128)(2,1)S(1)}, bf16[32,6,10,1]{0,1,3,2:T(8,128)(2,1)S(1)}, u32[]{:S(2)}, u32[]{:S(2)}) collective-permute-start(bf16[32,6,10,1]{0,1,3,2:T(8,128)(2,1)S(1)} %get-tuple-element.6), channel_id=1, source_target_pairs={{1,0},{3,2},{5,4},{7,6},{9,8},{11,10},{13,12},{15,14},{17,16},{19,... | collective-permute-start | bytes 11528 | tf_op jit(solution)/shard_map/ppermute | solution.py:17
  59.1 10.6 %copy-start.12 = (bf16[1,32,4,8,256]{4,1,3,2,0:T(8,128)(2,1)S(1)}, bf16[1,32,4,8,256]{4,1,3,2,0:T(8,128)(2,1)}, u32[]{:S(2)}) copy-start(bf16[1,32,4,8,256]{4,1,3,2,0:T(8,128)(2,1)} %get-tuple-element.41) | copy-start | bytes 1572868
  59.1 11.7 %copy-start.26 = (bf16[1,32,4,8,256]{4,1,3,2,0:T(8,128)(2,1)S(1)}, bf16[1,32,4,8,256]{4,1,3,2,0:T(8,128)(2,1)}, u32[]{:S(2)}) copy-start(bf16[1,32,4,8,256]{4,1,3,2,0:T(8,128)(2,1)} %get-tuple-element.63) | copy-start | bytes 1572868
  64.2 8.7 %copy-start.10 = (bf16[1,32,4,8,256]{4,1,3,2,0:T(8,128)(2,1)S(1)}, bf16[1,32,4,8,256]{4,1,3,2,0:T(8,128)(2,1)}, u32[]{:S(2)}) copy-start(bf16[1,32,4,8,256]{4,1,3,2,0:T(8,128)(2,1)} %get-tuple-element.44) | copy-start | bytes 1572868
  64.2 9.8 %copy-start.25 = (bf16[1,32,4,8,256]{4,1,3,2,0:T(8,128)(2,1)S(1)}, bf16[1,32,4,8,256]{4,1,3,2,0:T(8,128)(2,1)}, u32[]{:S(2)}) copy-start(bf16[1,32,4,8,256]{4,1,3,2,0:T(8,128)(2,1)} %get-tuple-element.65) | copy-start | bytes 1572868
  65.3 10.9 %copy-start.9 = (bf16[1,32,4,8,256]{4,1,3,2,0:T(8,128)(2,1)S(1)}, bf16[1,32,4,8,256]{4,1,3,2,0:T(8,128)(2,1)}, u32[]{:S(2)}) copy-start(bf16[1,32,4,8,256]{4,1,3,2,0:T(8,128)(2,1)} %get-tuple-element.47) | copy-start | bytes 1572868
  66.4 10.9 %copy-start.2 = (bf16[32,4,8,256]{3,2,1,0:T(8,128)(2,1)S(1)}, bf16[32,4,8,256]{3,2,1,0:T(8,128)(2,1)}, u32[]{:S(2)}) copy-start(bf16[32,4,8,256]{3,2,1,0:T(8,128)(2,1)} %param.6) | copy-start | bytes 1572868
  71.9 8.9 %copy-start.17 = (bf16[1,32,4,8,256]{4,1,3,2,0:T(8,128)(2,1)S(1)}, bf16[1,32,4,8,256]{4,1,3,2,0:T(8,128)(2,1)}, u32[]{:S(2)}) copy-start(bf16[1,32,4,8,256]{4,1,3,2,0:T(8,128)(2,1)} %get-tuple-element.39) | copy-start | bytes 1572868
  71.9 8.9 %copy-start.18 = (bf16[1,32,4,8,256]{4,1,3,2,0:T(8,128)(2,1)S(1)}, bf16[1,32,4,8,256]{4,1,3,2,0:T(8,128)(2,1)}, u32[]{:S(2)}) copy-start(bf16[1,32,4,8,256]{4,1,3,2,0:T(8,128)(2,1)} %get-tuple-element.45) | copy-start | bytes 1572868
  74.0 8.3 %copy-start.23 = (bf16[1,32,4,8,256]{4,1,3,2,0:T(8,128)(2,1)S(1)}, bf16[1,32,4,8,256]{4,1,3,2,0:T(8,128)(2,1)}, u32[]{:S(2)}) copy-start(bf16[1,32,4,8,256]{4,1,3,2,0:T(8,128)(2,1)} %get-tuple-element.54) | copy-start | bytes 1572868
  84.5 10.5 %copy-start.5 = (bf16[1,32,4,8,256]{4,1,3,2,0:T(8,128)(2,1)S(1)}, bf16[1,32,4,8,256]{4,1,3,2,0:T(8,128)(2,1)}, u32[]{:S(2)}) copy-start(bf16[1,32,4,8,256]{4,1,3,2,0:T(8,128)(2,1)} %get-tuple-element.36) | copy-start | bytes 1572868
  96.1 11.0 %copy-start.20 = (bf16[1,32,4,8,256]{4,1,3,2,0:T(8,128)(2,1)S(1)}, bf16[1,32,4,8,256]{4,1,3,2,0:T(8,128)(2,1)}, u32[]{:S(2)}) copy-start(bf16[1,32,4,8,256]{4,1,3,2,0:T(8,128)(2,1)} %get-tuple-element.55) | copy-start | bytes 1572868
  117.6 6.9 %slice-start.2 = ((s8[4718592]{0:T(1024)(128)(4,1)}), s8[4194304]{0:T(1024)(128)(4,1)S(1)}, s32[]{:S(2)}) async-start(s8[4718592]{0:T(1024)(128)(4,1)} %bitcast.207), calls=%async_computation.2 | async-start | bytes 8388608
  124.5 5.5 %copy-start.34 = (s32[4,1,1,256]{3,2,1,0:T(1,128)S(1)}, s32[4,1,1,256]{3,2,1,0:T(1,128)}, u32[]{:S(2)}) copy-start(s32[4,1,1,256]{3,2,1,0:T(1,128)} %param.10) | copy-start | bytes 12292
  124.5 6.1 %copy-start.31 = (bf16[32,3,3,32]{3,0,2,1:T(8,128)(2,1)S(1)}, bf16[32,3,3,32]{3,0,2,1:T(8,128)(2,1)}, u32[]{:S(2)}) copy-start(bf16[32,3,3,32]{3,0,2,1:T(8,128)(2,1)} %get-tuple-element.76) | copy-start | bytes 55300
  124.5 6.8 %copy-start.30 = (bf16[32,3,3,32]{3,0,2,1:T(8,128)(2,1)S(1)}, bf16[32,3,3,32]{3,0,2,1:T(8,128)(2,1)}, u32[]{:S(2)}) copy-start(bf16[32,3,3,32]{3,0,2,1:T(8,128)(2,1)} %get-tuple-element.77) | copy-start | bytes 55300
  124.6 7.7 %copy-start.36 = (s32[4,4]{1,0:T(4,128)S(1)}, s32[4,4]{1,0:T(4,128)}, u32[]{:S(2)}) copy-start(s32[4,4]{1,0:T(4,128)} %param.11) | copy-start | bytes 196
  125.7 8.0 %collective-permute-start.6 = (bf16[32,1,8,256]{3,2,1,0:T(8,128)(2,1)S(1)}, bf16[32,1,8,256]{3,2,1,0:T(8,128)(2,1)S(1)}, u32[]{:S(2)}, u32[]{:S(2)}) collective-permute-start(bf16[32,1,8,256]{3,2,1,0:T(8,128)(2,1)S(1)} %get-tuple-element.69), channel_id=1, source_target_pairs={{0,4},{4,8},{8,12},{1,5},{5,9},{9,13},{2,6},{6,10},{10,14},{3,7},{... | collective-permute-start | bytes 393224 | tf_op jit(solution)/shard_map/ppermute | solution.py:16
  132.3 8.1 %collective-permute-start.7 = (bf16[32,1,8,256]{3,2,1,0:T(8,128)(2,1)S(1)}, bf16[32,1,8,256]{3,2,1,0:T(8,128)(2,1)S(1)}, u32[]{:S(2)}, u32[]{:S(2)}) collective-permute-start(bf16[32,1,8,256]{3,2,1,0:T(8,128)(2,1)S(1)} %get-tuple-element.68), channel_id=1, source_target_pairs={{4,0},{8,4},{12,8},{5,1},{9,5},{13,9},{6,2},{10,6},{14,10},{7,3},{... | collective-permute-start | bytes 393224 | tf_op jit(solution)/shard_map/ppermute | solution.py:17
  140.5 26.0 %copy-start.28 = (bf16[32,1,8,256]{3,2,1,0:T(8,128)(2,1)}, bf16[32,1,8,256]{3,2,1,0:T(8,128)(2,1)S(1)}, u32[]{:S(2)}) copy-start(bf16[32,1,8,256]{3,2,1,0:T(8,128)(2,1)S(1)} %collective-permute-done.7) | copy-start | bytes 393220
  145.4 12.9 %collective-permute-start.8 = (bf16[32,6,1,256]{0,1,3,2:T(8,128)(2,1)S(1)}, bf16[32,6,1,256]{0,1,3,2:T(8,128)(2,1)S(1)}, u32[]{:S(2)}, u32[]{:S(2)}) collective-permute-start(bf16[32,6,1,256]{0,1,3,2:T(8,128)(2,1)S(1)} %get-tuple-element.8), channel_id=1, source_target_pairs={{0,2},{1,3},{4,6},{5,7},{8,10},{9,11},{12,14},{13,15},{16,18},{17,... | collective-permute-start | bytes 294920 | tf_op jit(solution)/shard_map/ppermute | solution.py:16
  147.0 15.4 %collective-permute-start.9 = (bf16[32,6,1,256]{0,1,3,2:T(8,128)(2,1)S(1)}, bf16[32,6,1,256]{0,1,3,2:T(8,128)(2,1)S(1)}, u32[]{:S(2)}, u32[]{:S(2)}) collective-permute-start(bf16[32,6,1,256]{0,1,3,2:T(8,128)(2,1)S(1)} %get-tuple-element.9), channel_id=1, source_target_pairs={{2,0},{3,1},{6,4},{7,5},{10,8},{11,9},{14,12},{15,13},{18,16},{19,... | collective-permute-start | bytes 294920 | tf_op jit(solution)/shard_map/ppermute | solution.py:17
  169.5 10.6 %collective-permute-start.10 = (bf16[32,6,10,1]{0,1,3,2:T(8,128)(2,1)}, bf16[32,6,10,1]{0,1,3,2:T(8,128)(2,1)S(1)}, u32[]{:S(2)}, u32[]{:S(2)}) collective-permute-start(bf16[32,6,10,1]{0,1,3,2:T(8,128)(2,1)} %get-tuple-element.5), channel_id=1, source_target_pairs={{0,1},{2,3},{4,5},{6,7},{8,9},{10,11},{12,13},{14,15},{16,17},{18,... | collective-permute-start | bytes 11528 | tf_op jit(solution)/shard_map/ppermute | solution.py:16
  170.7 14.6 %collective-permute-start.11 = (bf16[32,6,10,1]{0,1,3,2:T(8,128)(2,1)}, bf16[32,6,10,1]{0,1,3,2:T(8,128)(2,1)S(1)}, u32[]{:S(2)}, u32[]{:S(2)}) collective-permute-start(bf16[32,6,10,1]{0,1,3,2:T(8,128)(2,1)} %get-tuple-element.4), channel_id=1, source_target_pairs={{1,0},{3,2},{5,4},{7,6},{9,8},{11,10},{13,12},{15,14},{17,16},{19,... | collective-permute-start | bytes 11528 | tf_op jit(solution)/shard_map/ppermute | solution.py:17
  186.5 5.4 %copy-start.16 = (bf16[1,32,4,8,256]{4,1,3,2,0:T(8,128)(2,1)S(1)}, bf16[1,32,4,8,256]{4,1,3,2,0:T(8,128)(2,1)}, u32[]{:S(2)}) copy-start(bf16[1,32,4,8,256]{4,1,3,2,0:T(8,128)(2,1)} %get-tuple-element.28) | copy-start | bytes 1572868
  186.5 9.8 %copy-start.13 = (bf16[1,32,4,8,256]{4,1,3,2,0:T(8,128)(2,1)S(1)}, bf16[1,32,4,8,256]{4,1,3,2,0:T(8,128)(2,1)}, u32[]{:S(2)}) copy-start(bf16[1,32,4,8,256]{4,1,3,2,0:T(8,128)(2,1)} %get-tuple-element.23) | copy-start | bytes 1572868
  186.5 10.9 %copy-start.27 = (bf16[1,32,4,8,256]{4,1,3,2,0:T(8,128)(2,1)S(1)}, bf16[1,32,4,8,256]{4,1,3,2,0:T(8,128)(2,1)}, u32[]{:S(2)}) copy-start(bf16[1,32,4,8,256]{4,1,3,2,0:T(8,128)(2,1)} %get-tuple-element.62) | copy-start | bytes 1572868
  186.5 13.1 %copy-start.11 = (bf16[1,32,4,8,256]{4,1,3,2,0:T(8,128)(2,1)S(1)}, bf16[1,32,4,8,256]{4,1,3,2,0:T(8,128)(2,1)}, u32[]{:S(2)}) copy-start(bf16[1,32,4,8,256]{4,1,3,2,0:T(8,128)(2,1)} %get-tuple-element.29) | copy-start | bytes 1572868
  192.0 8.7 %copy-start.29 = (bf16[32,1,8,256]{3,2,1,0:T(8,128)(2,1)S(1)}, bf16[32,1,8,256]{3,2,1,0:T(8,128)(2,1)}, u32[]{:S(2)}) copy-start(bf16[32,1,8,256]{3,2,1,0:T(8,128)(2,1)} %copy-done.28) | copy-start | bytes 393220
  193.1 9.9 %copy-start.8 = (bf16[1,32,4,8,256]{4,1,3,2,0:T(8,128)(2,1)S(1)}, bf16[1,32,4,8,256]{4,1,3,2,0:T(8,128)(2,1)}, u32[]{:S(2)}) copy-start(bf16[1,32,4,8,256]{4,1,3,2,0:T(8,128)(2,1)} %get-tuple-element.21) | copy-start | bytes 1572868
  195.2 8.8 %copy-start.24 = (bf16[1,32,4,8,256]{4,1,3,2,0:T(8,128)(2,1)S(1)}, bf16[1,32,4,8,256]{4,1,3,2,0:T(8,128)(2,1)}, u32[]{:S(2)}) copy-start(bf16[1,32,4,8,256]{4,1,3,2,0:T(8,128)(2,1)} %get-tuple-element.48) | copy-start | bytes 1572868
  214.5 9.5 %copy-start.7 = (bf16[1,32,4,8,256]{4,1,3,2,0:T(8,128)(2,1)S(1)}, bf16[1,32,4,8,256]{4,1,3,2,0:T(8,128)(2,1)}, u32[]{:S(2)}) copy-start(bf16[1,32,4,8,256]{4,1,3,2,0:T(8,128)(2,1)} %get-tuple-element.17) | copy-start | bytes 1572868
  214.5 10.6 %copy-start.3 = (bf16[1,32,4,8,256]{4,1,3,2,0:T(8,128)(2,1)S(1)}, bf16[1,32,4,8,256]{4,1,3,2,0:T(8,128)(2,1)}, u32[]{:S(2)}) copy-start(bf16[1,32,4,8,256]{4,1,3,2,0:T(8,128)(2,1)} %get-tuple-element.27) | copy-start | bytes 1572868
  214.5 11.7 %copy-start.22 = (bf16[1,32,4,8,256]{4,1,3,2,0:T(8,128)(2,1)S(1)}, bf16[1,32,4,8,256]{4,1,3,2,0:T(8,128)(2,1)}, u32[]{:S(2)}) copy-start(bf16[1,32,4,8,256]{4,1,3,2,0:T(8,128)(2,1)} %get-tuple-element.50) | copy-start | bytes 1572868
  214.5 12.8 %copy-start.6 = (bf16[1,32,4,8,256]{4,1,3,2,0:T(8,128)(2,1)S(1)}, bf16[1,32,4,8,256]{4,1,3,2,0:T(8,128)(2,1)}, u32[]{:S(2)}) copy-start(bf16[1,32,4,8,256]{4,1,3,2,0:T(8,128)(2,1)} %get-tuple-element.18) | copy-start | bytes 1572868
  228.4 8.6 %copy-start.4 = (bf16[1,32,4,8,256]{4,1,3,2,0:T(8,128)(2,1)S(1)}, bf16[1,32,4,8,256]{4,1,3,2,0:T(8,128)(2,1)}, u32[]{:S(2)}) copy-start(bf16[1,32,4,8,256]{4,1,3,2,0:T(8,128)(2,1)} %get-tuple-element.14) | copy-start | bytes 1572868
  228.4 10.8 %copy-start.21 = (bf16[1,32,4,8,256]{4,1,3,2,0:T(8,128)(2,1)S(1)}, bf16[1,32,4,8,256]{4,1,3,2,0:T(8,128)(2,1)}, u32[]{:S(2)}) copy-start(bf16[1,32,4,8,256]{4,1,3,2,0:T(8,128)(2,1)} %get-tuple-element.49) | copy-start | bytes 1572868
  241.3 8.3 %copy-start.32 = (bf16[32,288]{1,0:T(8,128)(2,1)S(1)}, bf16[32,288]{1,0:T(8,128)(2,1)}, u32[]{:S(2)}) copy-start(bf16[32,288]{1,0:T(8,128)(2,1)} %reshape.198) | copy-start | bytes 55300
  249.6 6.9 %slice-start = ((s8[4718592]{0:T(1024)(128)(4,1)}), s8[4194304]{0:T(1024)(128)(4,1)S(1)}, s32[]{:S(2)}) async-start(s8[4718592]{0:T(1024)(128)(4,1)} %bitcast.205), calls=%async_computation | async-start | bytes 8388608
  257.6 16.0 %copy-start.38 = (s32[1,1,1,256]{3,2,1,0:T(1,128)S(1)}, s32[1,1,1,256]{3,2,1,0:T(1,128)}, u32[]{:S(2)}) copy-start(s32[1,1,1,256]{3,2,1,0:T(1,128)} %constant_dynamic-slice_fusion) | copy-start | bytes 3076
  257.6 16.0 %copy-start.39 = (f32[4]{0:T(128)S(1)}, f32[4]{0:T(128)}, u32[]{:S(2)}) copy-start(f32[4]{0:T(128)} %dynamic-slice_bitcast_fusion) | copy-start | bytes 52
  258.1 16.6 %copy-start.19 = (bf16[32,4,8,256]{3,2,1,0:T(8,128)(2,1)}, bf16[32,4,8,256]{3,2,1,0:T(8,128)(2,1)S(1)}, u32[]{:S(2)}) copy-start(bf16[32,4,8,256]{3,2,1,0:T(8,128)(2,1)S(1)} %add_convert_fusion) | copy-start | bytes 1572868
  (8 other events, 26.9 us)
where the time goes:
time: 280 us; the launch traced here: 275 us
  local copies, waits for them, and re-layouts  153 us (55%)
  other arithmetic  33.5 us (12%)
  waiting for transfers between devices  32.7 us (12%)
  starting transfers between devices  24.8 us (9%)
  matrix products  16.3 us (6%)
  blocking collectives  13.4 us (5%)
    unnamed x137, local copies, waits for them, and re-layouts  59.9 us
    reshape x6, local copies, waits for them, and re-layouts, conv_valid(): patches = stacked.reshape(9 * channels, out_z * out_y * out_x)  50.6 us
    another operation x6, other arithmetic, conv_valid(): jnp.stack([plane[:, :, offset_y:offset_y + out_y, column_shift:column_shi...  21.2 us
    concatenate x8, local copies, waits for them, and re-layouts, extended(): shard = jnp.concatenate([before, shard, after], axis=dim)  16.8 us
    ppermute x6, starting transfers between devices, extended(): before = lax.ppermute(last, axis, up)  16.8 us
    ppermute x6, waiting for transfers between devices, extended(): before = lax.ppermute(last, axis, up)  16.6 us
    ppermute x6, waiting for transfers between devices, extended(): after = lax.ppermute(leading, axis, down)  16 us
    dot_general x6, matrix products, conv_valid(): jnp.dot(kernel, patches, preferred_element_type=jnp.float32)  15.8 us
  transfers between devices with their start and end apart: 12, of which 7 were waited for; matrix products, arithmetic and copies ran while one was open for 12% of the time, Pallas kernels for 0%

commit v1 on v0

--- a/solution.py
+++ b/solution.py
@@ -47,6 +47,30 @@
 
 
 def shards(volume, first_weight, second_weight, sample_index, segments, block_match):
+
+    def tell_the_group(x0, axis_name, incoming_x):
+        part_now, big, state_now = (
+            lax.psum(1, axis_name=axis_name),
+            lax.axis_index(axis_name),
+            x0.shape[0],
+        )
+        kept_rows = []
+        for no in range(part_now):
+            block_now = (
+                lax.ppermute(
+                    x0,
+                    axis_name=axis_name,
+                    perm=[(ii, (ii + 1) % part_now) for ii in range(part_now)],
+                )
+                if no + 1 < part_now
+                else x0
+            )
+            kept_rows.append(incoming_x(x0, (big - no) % part_now * state_now))
+            x0 = block_now
+        outer = jnp.concatenate(kept_rows[::-1], axis=1)
+        z = jnp.roll(outer, shift=(big + 1) * kept_rows[0].shape[1], axis=1)
+        return z
+
     channels, slab_depth, tile_height, tile_width = volume.shape
     hidden = jax.nn.relu(conv_valid(pad_layer(volume), first_weight)).astype(jnp.bfloat16)
     conv_out = conv_valid(pad_layer(hidden), second_weight)
@@ -62,11 +86,12 @@
     rows = embedding.shape[1]
     match_row = lax.dynamic_index_in_dim(match_float, own_block, 0, keepdims=False)
     similarity_logits = (
-        jnp.einsum(
-            "cr,kcs->rks",
-            embedding,
-            lax.all_gather(query_rows, "gz", axis=0, tiled=True),
-            preferred_element_type=jnp.float32,
+        tell_the_group(
+            query_rows,
+            "gz",
+            lambda own_block_2, at: jnp.einsum(
+                "cr,kcs->rks", embedding, own_block_2, preferred_element_type=jnp.float32
+            ),
         )
         / SOFTMAX_WARMTH
     )

time: 280 us -> 287 us (1.025)
  waiting for transfers between devices: 32.7 us -> 51.4 us
  blocking collectives: 13.4 us -> 0 us
    ppermute x0 -> x3, waiting for transfers between devices: none -> 16.8 us  [tell_the_group(): lax.ppermute(x0, axis_name=axis_name, perm=[(ii, (ii + 1) % part_now) for...]
    all_gather x1 -> x0, blocking collectives: 13.4 us -> none  [shards(): lax.all_gather(query_rows, 'gz', axis=0, tiled=True)]
    unnamed x137 -> x128, local copies, waits for them, and re-layouts: 59.9 us -> 60.3 us
  transfers between devices with their start and end apart: 12 -> 15, of which waited for: 7 -> 10; matrix products, arithmetic and copies ran while one was open for 12% -> 11% of each run, Pallas kernels for 0% -> 0%
where the time goes in v1:
time: 287 us; the launch traced here: 281 us
  local copies, waits for them, and re-layouts  152 us (53%)
  waiting for transfers between devices  51.4 us (18%)
  other arithmetic  33.4 us (12%)
  starting transfers between devices  26.2 us (9%)
  matrix products  17 us (6%)
    unnamed x128, local copies, waits for them, and re-layouts  60.3 us
    reshape x6, local copies, waits for them, and re-layouts, conv_valid(): patches = stacked.reshape(9 * channels, out_z * out_y * out_x)  50.6 us
    another operation x6, other arithmetic, conv_valid(): jnp.stack([plane[:, :, offset_y:offset_y + out_y, column_shift:column_shi...  21.3 us
    ppermute x6, waiting for transfers between devices, extended(): before = lax.ppermute(last, axis, up)  19 us
    ppermute x3, waiting for transfers between devices, tell_the_group(): lax.ppermute(x0, axis_name=axis_name, perm=[(ii, (ii + 1) % part_now) for...  16.8 us
    concatenate x8, local copies, waits for them, and re-layouts, extended(): shard = jnp.concatenate([before, shard, after], axis=dim)  16.8 us
    ppermute x6, starting transfers between devices, extended(): before = lax.ppermute(last, axis, up)  16.6 us
    dot_general x6, matrix products, conv_valid(): jnp.dot(kernel, patches, preferred_element_type=jnp.float32)  15.8 us
  transfers between devices with their start and end apart: 15, of which 10 were waited for; matrix products, arithmetic and copies ran while one was open for 11% of the time, Pallas kernels for 0%

profile of v1, /device:TPU:0, one launch (start us, length us, event | category | flops | bytes accessed | tf_op | source)
XLA Modules:
  0.0 281.2 jit_solution(10569204852346299382)
XLA Ops:
  1.6 4.9 %collective-permute-start = (bf16[32,1,8,256]{3,2,1,0:T(8,128)(2,1)S(1)}, bf16[32,1,8,256]{3,2,1,0:T(8,128)(2,1)S(1)}, u32[]{:S(2)}, u32[]{:S(2)}) collective-permute-start(bf16[32,1,8,256]{3,2,1,0:T(8,128)(2,1)S(1)} %get-tuple-element.74), channel_id=1, source_target_pairs={{0,4},{4,8},{8,12},{1,5},{5,9},{9,13},{2,6},{6,10},{10,14},{3,7},{... | collective-permute-start | bytes 393224 | tf_op jit(solution)/shard_map/ppermute | solution.py:16
  10.9 2.5 collective-permute-done.1
  13.5 3.5 %copy.137 = bf16[32,6,8,256]{0,1,3,2:T(8,128)(2,1)} copy(bf16[32,6,8,256]{3,2,1,0:T(8,128)(2,1)S(1)} %constant_dynamic-update-slice_fusion) | data formatting | bytes 1572864 | tf_op jit(solution)/shard_map/concatenate | solution.py:18
  17.0 2.4 fusion.112
  19.3 3.4 %collective-permute-start.2 = (bf16[32,6,1,256]{0,1,3,2:T(8,128)(2,1)}, bf16[32,6,1,256]{0,1,3,2:T(8,128)(2,1)S(1)}, u32[]{:S(2)}, u32[]{:S(2)}) collective-permute-start(bf16[32,6,1,256]{0,1,3,2:T(8,128)(2,1)} %get-tuple-element.10), channel_id=1, source_target_pairs={{0,2},{1,3},{4,6},{5,7},{8,10},{9,11},{12,14},{13,15},{16,18},{17,... | collective-permute-start | bytes 294920 | tf_op jit(solution)/shard_map/ppermute | solution.py:16
  25.4 7.4 %collective-permute-done.2 = bf16[32,6,1,256]{0,1,3,2:T(8,128)(2,1)S(1)} collective-permute-done((bf16[32,6,1,256]{0,1,3,2:T(8,128)(2,1)}, bf16[32,6,1,256]{0,1,3,2:T(8,128)(2,1)S(1)}, u32[]{:S(2)}, u32[]{:S(2)}) %collective-permute-start.2) | collective-permute-done | bytes 98336 | tf_op jit(solution)/shard_map/ppermute | solution.py:16
  32.8 4.0 %collective-permute-done.3 = bf16[32,6,1,256]{0,1,3,2:T(8,128)(2,1)S(1)} collective-permute-done((bf16[32,6,1,256]{0,1,3,2:T(8,128)(2,1)}, bf16[32,6,1,256]{0,1,3,2:T(8,128)(2,1)S(1)}, u32[]{:S(2)}, u32[]{:S(2)}) %collective-permute-start.3) | collective-permute-done | bytes 98336 | tf_op jit(solution)/shard_map/ppermute | solution.py:17
  36.8 3.8 %pad_maximum_fusion = bf16[32,6,10,256]{0,1,3,2:T(8,128)(2,1)S(1)} fusion(bf16[32,6,1,256]{0,1,3,2:T(8,128)(2,1)S(1)} %collective-permute-done.3, bf16[32,6,8,256]{0,1,3,2:T(8,128)(2,1)} %copy.137, bf16[32,6,1,256]{0,1,3,2:T(8,128)(2,1)S(1)} %collective-permute-done.2), kind=kLoop, calls=%fused_computation.7 | loop fusion | flops 983040 | bytes 1966080 | tf_op jit(solution)/shard_map/concatenate | solution.py:18
  40.7 2.3 copy-done
  46.5 1.7 fusion.92
  48.2 4.5 %copy.141 = bf16[32,6,10,256]{3,0,2,1:T(8,128)(2,1)S(1)} copy(bf16[32,6,10,256]{0,1,3,2:T(8,128)(2,1)} %copy-done) | data formatting | bytes 1966080 | tf_op jit(solution)/shard_map/concatenate | solution.py:18
  53.2 3.6 %fusion.93 = (bf16[1,32,4,8,256]{4,1,3,2,0:T(8,128)(2,1)}, bf16[1,32,4,8,256]{4,1,3,2,0:T(8,128)(2,1)S(1)}, bf16[1,32,4,8,256]{4,1,3,2,0:T(8,128)(2,1)}, bf16[1,...) fusion(bf16[32,6,10,256]{3,0,2,1:T(8,128)(2,1)S(1)} %copy.141, ...), kind=kLoop, calls=%fused_computation.196 | loop fusion | flops 9437184 | bytes 5705472 | tf_op jit(solution)/shard_map/stack | solution.py:31
  59.1 5.1 %fusion.91 = (bf16[1,32,4,8,256]{4,1,3,2,0:T(8,128)(2,1)S(1)}, bf16[1,32,4,8,256]{4,1,3,2,0:T(8,128)(2,1)S(1)}, bf16[1,32,4,8,256]{4,1,3,2,0:T(8,128)(2,1)S(1)},...) fusion(bf16[32,6,10,1]{3,0,2,1:T(8,128)(2,1)} %copy.145, ...), kind=kLoop, calls=%fused_computation.192 | loop fusion | flops 9437184 | bytes 5705472 | tf_op jit(solution)/shard_map/stack | solution.py:31
  66.5 2.2 copy_dynamic-update-slice_fusion.46
  84.6 8.4 %reshape.217 = bf16[288,8192]{1,0:T(8,128)(2,1)} reshape(bf16[9,32,4,8,256]{4,3,2,1,0:T(8,128)(2,1)} %copy_dynamic-update-slice_fusion.24) | data formatting | bytes 9437184 | tf_op jit(solution)/shard_map/reshape | solution.py:39
  93.0 2.1 copy_dynamic-update-slice_fusion.33
  96.2 8.8 %reshape.215 = bf16[288,8192]{1,0:T(8,128)(2,1)} reshape(bf16[9,32,4,8,256]{4,3,2,1,0:T(8,128)(2,1)} %copy_dynamic-update-slice_fusion.32) | data formatting | bytes 9437184 | tf_op jit(solution)/shard_map/reshape | solution.py:39
  109.4 8.3 %reshape.213 = bf16[288,8192]{1,0:T(8,128)(2,1)} reshape(bf16[9,32,4,8,256]{4,3,2,1,0:T(8,128)(2,1)} %copy_dynamic-update-slice_fusion.40) | data formatting | bytes 9437184 | tf_op jit(solution)/shard_map/reshape | solution.py:39
  117.7 3.5 %fusion.115 = f32[8192,32]{0,1:T(8,128)S(1)} fusion(bf16[32,288]{1,0:T(8,128)(2,1)S(1)} %reshape.214, bf16[288,8192]{1,0:T(8,128)(2,1)} %reshape.213), kind=kOutput, calls=%fused_computation.301 | convolution fusion | flops 150994944 | bytes 5785600 | tf_op jit(solution)/shard_map/dot_general | solution.py:41
  121.2 3.4 %convolution_add_fusion.3 = f32[8192,32]{0,1:T(8,128)S(1)} fusion(f32[8192,32]{0,1:T(8,128)S(1)} %fusion.115, bf16[32,288]{1,0:T(8,128)(2,1)S(1)} %reshape.216, bf16[288,8192]{1,0:T(8,128)(2,1)} %reshape.215), kind=kOutput, calls=%fused_computation.5 | convolution fusion | flops 151257088 | bytes 6834176 | tf_op jit(solution)/shard_map/dot_general | solution.py:41
  125.8 3.5 %collective-permute-start.6 = (bf16[32,1,8,256]{3,2,1,0:T(8,128)(2,1)S(1)}, bf16[32,1,8,256]{3,2,1,0:T(8,128)(2,1)S(1)}, u32[]{:S(2)}, u32[]{:S(2)}) collective-permute-start(bf16[32,1,8,256]{3,2,1,0:T(8,128)(2,1)S(1)} %get-tuple-element.69), channel_id=1, source_target_pairs={{0,4},{4,8},{8,12},{1,5},{5,9},{9,13},{2,6},{6,10},{10,14},{3,7},{... | collective-permute-start | bytes 393224 | tf_op jit(solution)/shard_map/ppermute | solution.py:16
  131.1 1.9 collective-permute-done.6
  133.1 4.9 %collective-permute-done.7 = bf16[32,1,8,256]{3,2,1,0:T(8,128)(2,1)S(1)} collective-permute-done((bf16[32,1,8,256]{3,2,1,0:T(8,128)(2,1)S(1)}, bf16[32,1,8,256]{3,2,1,0:T(8,128)(2,1)S(1)}, u32[]{:S(2)}, u32[]{:S(2)}) %collective-permute-start.7) | collective-permute-done | bytes 131104 | tf_op jit(solution)/shard_map/ppermute | solution.py:17
  138.0 3.5 %copy.175 = bf16[32,6,8,256]{0,1,3,2:T(8,128)(2,1)} copy(bf16[32,6,8,256]{3,2,1,0:T(8,128)(2,1)S(1)} %constant_dynamic-update-slice_fusion.3) | data formatting | bytes 1572864 | tf_op jit(solution)/shard_map/concatenate | solution.py:18
  146.1 9.7 %collective-permute-done.8 = bf16[32,6,1,256]{0,1,3,2:T(8,128)(2,1)S(1)} collective-permute-done((bf16[32,6,1,256]{0,1,3,2:T(8,128)(2,1)S(1)}, bf16[32,6,1,256]{0,1,3,2:T(8,128)(2,1)S(1)}, u32[]{:S(2)}, u32[]{:S(2)}) %collective-permute-start.8) | collective-permute-done | bytes 98336 | tf_op jit(solution)/shard_map/ppermute | solution.py:16
  155.8 4.1 %collective-permute-done.9 = bf16[32,6,1,256]{0,1,3,2:T(8,128)(2,1)S(1)} collective-permute-done((bf16[32,6,1,256]{0,1,3,2:T(8,128)(2,1)S(1)}, bf16[32,6,1,256]{0,1,3,2:T(8,128)(2,1)S(1)}, u32[]{:S(2)}, u32[]{:S(2)}) %collective-permute-start.9) | collective-permute-done | bytes 98336 | tf_op jit(solution)/shard_map/ppermute | solution.py:17
  159.9 4.0 %pad_maximum_fusion.1 = bf16[32,6,10,256]{0,1,3,2:T(8,128)(2,1)S(1)} fusion(bf16[32,6,1,256]{0,1,3,2:T(8,128)(2,1)S(1)} %collective-permute-done.9, bf16[32,6,8,256]{0,1,3,2:T(8,128)(2,1)} %copy.175, bf16[32,6,1,256]{0,1,3,2:T(8,128)(2,1)S(1)} %collective-permute-done.8), kind=kLoop, calls=%fused_computation.8 | loop fusion | flops 983040 | bytes 1966080 | tf_op jit(solution)/shard_map/concatenate | solution.py:18
  164.0 2.3 copy-done.1
  167.0 1.9 collective-permute-start.10
  171.7 1.8 fusion.84
  173.5 4.7 %copy.179 = bf16[32,6,10,256]{3,0,2,1:T(8,128)(2,1)S(1)} copy(bf16[32,6,10,256]{0,1,3,2:T(8,128)(2,1)} %copy-done.1) | data formatting | bytes 1966080 | tf_op jit(solution)/shard_map/concatenate | solution.py:18
  179.4 3.7 %fusion.85 = (bf16[1,32,4,8,256]{4,1,3,2,0:T(8,128)(2,1)}, bf16[1,32,4,8,256]{4,1,3,2,0:T(8,128)(2,1)S(1)}, bf16[1,32,4,8,256]{4,1,3,2,0:T(8,128)(2,1)}, bf16[1,...) fusion(bf16[32,6,10,256]{3,0,2,1:T(8,128)(2,1)S(1)} %copy.179, ...), kind=kLoop, calls=%fused_computation.182 | loop fusion | flops 9437184 | bytes 5705472 | tf_op jit(solution)/shard_map/stack | solution.py:31
  184.2 1.9 copy.183
  186.1 5.5 %fusion.83 = (bf16[1,32,4,8,256]{4,1,3,2,0:T(8,128)(2,1)S(1)}, bf16[1,32,4,8,256]{4,1,3,2,0:T(8,128)(2,1)S(1)}, bf16[1,32,4,8,256]{4,1,3,2,0:T(8,128)(2,1)}, bf1...) fusion(bf16[32,6,10,1]{3,0,2,1:T(8,128)(2,1)} %copy.183, ...), kind=kLoop, calls=%fused_computation.178 | loop fusion | flops 9437184 | bytes 5705472 | tf_op jit(solution)/shard_map/stack | solution.py:31
  192.7 2.2 copy_dynamic-update-slice_fusion.22
  205.9 8.3 %reshape.223 = bf16[288,8192]{1,0:T(8,128)(2,1)} reshape(bf16[9,32,4,8,256]{4,3,2,1,0:T(8,128)(2,1)} %copy_dynamic-update-slice_fusion) | data formatting | bytes 9437184 | tf_op jit(solution)/shard_map/reshape | solution.py:39
  214.2 2.3 copy_dynamic-update-slice_fusion.15
  216.5 2.1 copy_dynamic-update-slice_fusion.14
  218.6 2.2 copy_dynamic-update-slice_fusion.13
  220.7 2.1 copy_dynamic-update-slice_fusion.12
  228.1 8.5 %reshape.221 = bf16[288,8192]{1,0:T(8,128)(2,1)} reshape(bf16[9,32,4,8,256]{4,3,2,1,0:T(8,128)(2,1)} %copy_dynamic-update-slice_fusion.8) | data formatting | bytes 9437184 | tf_op jit(solution)/shard_map/reshape | solution.py:39
  241.0 8.3 %reshape.219 = bf16[288,8192]{1,0:T(8,128)(2,1)} reshape(bf16[9,32,4,8,256]{4,3,2,1,0:T(8,128)(2,1)} %copy_dynamic-update-slice_fusion.16) | data formatting | bytes 9437184 | tf_op jit(solution)/shard_map/reshape | solution.py:39
  249.3 3.5 %fusion.116 = f32[8192,32]{0,1:T(8,128)S(1)} fusion(bf16[32,288]{1,0:T(8,128)(2,1)S(1)} %reshape.220, bf16[288,8192]{1,0:T(8,128)(2,1)} %reshape.219), kind=kOutput, calls=%fused_computation.302 | convolution fusion | flops 150994944 | bytes 5785600 | tf_op jit(solution)/shard_map/dot_general | solution.py:41
  252.8 3.4 %convolution_add_fusion.1 = f32[8192,32]{0,1:T(8,128)S(1)} fusion(f32[8192,32]{0,1:T(8,128)S(1)} %fusion.116, bf16[32,288]{1,0:T(8,128)(2,1)S(1)} %reshape.222, bf16[288,8192]{1,0:T(8,128)(2,1)} %reshape.221), kind=kOutput, calls=%fused_computation.2 | convolution fusion | flops 151257088 | bytes 6834176 | tf_op jit(solution)/shard_map/dot_general | solution.py:41
  260.2 1.6 collective-permute-start.12
  261.8 4.5 %collective-permute-done.12 = bf16[1,32,256]{1,2,0:T(8,128)(2,1)S(1)} collective-permute-done((bf16[1,32,256]{1,2,0:T(8,128)(2,1)S(1)}, bf16[1,32,256]{1,2,0:T(8,128)(2,1)S(1)}, u32[]{:S(2)}, u32[]{:S(2)}) %collective-permute-start.12) | collective-permute-done | bytes 16416 | tf_op jit(solution)/shard_map/ppermute | solution.py:60
  266.3 6.3 %collective-permute-done.13 = bf16[1,32,256]{1,2,0:T(8,128)(2,1)S(1)} collective-permute-done((bf16[1,32,256]{1,2,0:T(8,128)(2,1)S(1)}, bf16[1,32,256]{1,2,0:T(8,128)(2,1)S(1)}, u32[]{:S(2)}, u32[]{:S(2)}) %collective-permute-start.13) | collective-permute-done | bytes 16416 | tf_op jit(solution)/shard_map/ppermute | solution.py:60
  272.7 6.0 %collective-permute-done.14 = bf16[1,32,256]{1,2,0:T(8,128)(2,1)S(1)} collective-permute-done((bf16[1,32,256]{1,2,0:T(8,128)(2,1)S(1)}, bf16[1,32,256]{1,2,0:T(8,128)(2,1)S(1)}, u32[]{:S(2)}, u32[]{:S(2)}) %collective-permute-start.14) | collective-permute-done | bytes 16416 | tf_op jit(solution)/shard_map/ppermute | solution.py:60
  (195 shorter events, 78.8 us)
Async XLA Ops:
  1.6 8.2 %collective-permute-start = (bf16[32,1,8,256]{3,2,1,0:T(8,128)(2,1)S(1)}, bf16[32,1,8,256]{3,2,1,0:T(8,128)(2,1)S(1)}, u32[]{:S(2)}, u32[]{:S(2)}) collective-permute-start(bf16[32,1,8,256]{3,2,1,0:T(8,128)(2,1)S(1)} %get-tuple-element.74), channel_id=1, source_target_pairs={{0,4},{4,8},{8,12},{1,5},{5,9},{9,13},{2,6},{6,10},{10,14},{3,7},{... | collective-permute-start | bytes 393224 | tf_op jit(solution)/shard_map/ppermute | solution.py:16
  6.6 17.5 %copy-start.33 = (s32[1,1,1,256]{3,2,1,0:T(1,128)S(1)}, s32[1,1,1,256]{3,2,1,0:T(1,128)}, u32[]{:S(2)}) copy-start(s32[1,1,1,256]{3,2,1,0:T(1,128)} %param.9) | copy-start | bytes 3076
  6.6 6.9 %collective-permute-start.1 = (bf16[32,1,8,256]{3,2,1,0:T(8,128)(2,1)S(1)}, bf16[32,1,8,256]{3,2,1,0:T(8,128)(2,1)S(1)}, u32[]{:S(2)}, u32[]{:S(2)}) collective-permute-start(bf16[32,1,8,256]{3,2,1,0:T(8,128)(2,1)S(1)} %get-tuple-element.73), channel_id=1, source_target_pairs={{4,0},{8,4},{12,8},{5,1},{9,5},{13,9},{6,2},{10,6},{14,10},{7,3},{... | collective-permute-start | bytes 393224 | tf_op jit(solution)/shard_map/ppermute | solution.py:17
  19.3 13.4 %collective-permute-start.2 = (bf16[32,6,1,256]{0,1,3,2:T(8,128)(2,1)}, bf16[32,6,1,256]{0,1,3,2:T(8,128)(2,1)S(1)}, u32[]{:S(2)}, u32[]{:S(2)}) collective-permute-start(bf16[32,6,1,256]{0,1,3,2:T(8,128)(2,1)} %get-tuple-element.10), channel_id=1, source_target_pairs={{0,2},{1,3},{4,6},{5,7},{8,10},{9,11},{12,14},{13,15},{16,18},{17,... | collective-permute-start | bytes 294920 | tf_op jit(solution)/shard_map/ppermute | solution.py:16
  22.8 14.1 %collective-permute-start.3 = (bf16[32,6,1,256]{0,1,3,2:T(8,128)(2,1)}, bf16[32,6,1,256]{0,1,3,2:T(8,128)(2,1)S(1)}, u32[]{:S(2)}, u32[]{:S(2)}) collective-permute-start(bf16[32,6,1,256]{0,1,3,2:T(8,128)(2,1)} %get-tuple-element.11), channel_id=1, source_target_pairs={{2,0},{3,1},{6,4},{7,5},{10,8},{11,9},{14,12},{15,13},{18,16},{19,... | collective-permute-start | bytes 294920 | tf_op jit(solution)/shard_map/ppermute | solution.py:17
  43.0 9.7 %collective-permute-start.4 = (bf16[32,6,10,1]{0,1,3,2:T(8,128)(2,1)S(1)}, bf16[32,6,10,1]{0,1,3,2:T(8,128)(2,1)S(1)}, u32[]{:S(2)}, u32[]{:S(2)}) collective-permute-start(bf16[32,6,10,1]{0,1,3,2:T(8,128)(2,1)S(1)} %get-tuple-element.7), channel_id=1, source_target_pairs={{0,1},{2,3},{4,5},{6,7},{8,9},{10,11},{12,13},{14,15},{16,17},{18,... | collective-permute-start | bytes 11528 | tf_op jit(solution)/shard_map/ppermute | solution.py:16
  44.3 13.6 %collective-permute-start.5 = (bf16[32,6,10,1]{0,1,3,2:T(8,128)(2,1)S(1)}, bf16[32,6,10,1]{0,1,3,2:T(8,128)(2,1)S(1)}, u32[]{:S(2)}, u32[]{:S(2)}) collective-permute-start(bf16[32,6,10,1]{0,1,3,2:T(8,128)(2,1)S(1)} %get-tuple-element.6), channel_id=1, source_target_pairs={{1,0},{3,2},{5,4},{7,6},{9,8},{11,10},{13,12},{15,14},{17,16},{19,... | collective-permute-start | bytes 11528 | tf_op jit(solution)/shard_map/ppermute | solution.py:17
  59.1 5.1 %copy-start.14 = (bf16[1,32,4,8,256]{4,1,3,2,0:T(8,128)(2,1)S(1)}, bf16[1,32,4,8,256]{4,1,3,2,0:T(8,128)(2,1)}, u32[]{:S(2)}) copy-start(bf16[1,32,4,8,256]{4,1,3,2,0:T(8,128)(2,1)} %get-tuple-element.43) | copy-start | bytes 1572868
  59.1 10.7 %copy-start.12 = (bf16[1,32,4,8,256]{4,1,3,2,0:T(8,128)(2,1)S(1)}, bf16[1,32,4,8,256]{4,1,3,2,0:T(8,128)(2,1)}, u32[]{:S(2)}) copy-start(bf16[1,32,4,8,256]{4,1,3,2,0:T(8,128)(2,1)} %get-tuple-element.41) | copy-start | bytes 1572868
  59.1 11.8 %copy-start.26 = (bf16[1,32,4,8,256]{4,1,3,2,0:T(8,128)(2,1)S(1)}, bf16[1,32,4,8,256]{4,1,3,2,0:T(8,128)(2,1)}, u32[]{:S(2)}) copy-start(bf16[1,32,4,8,256]{4,1,3,2,0:T(8,128)(2,1)} %get-tuple-element.63) | copy-start | bytes 1572868
  64.2 8.8 %copy-start.10 = (bf16[1,32,4,8,256]{4,1,3,2,0:T(8,128)(2,1)S(1)}, bf16[1,32,4,8,256]{4,1,3,2,0:T(8,128)(2,1)}, u32[]{:S(2)}) copy-start(bf16[1,32,4,8,256]{4,1,3,2,0:T(8,128)(2,1)} %get-tuple-element.44) | copy-start | bytes 1572868
  64.2 9.9 %copy-start.25 = (bf16[1,32,4,8,256]{4,1,3,2,0:T(8,128)(2,1)S(1)}, bf16[1,32,4,8,256]{4,1,3,2,0:T(8,128)(2,1)}, u32[]{:S(2)}) copy-start(bf16[1,32,4,8,256]{4,1,3,2,0:T(8,128)(2,1)} %get-tuple-element.65) | copy-start | bytes 1572868
  65.4 11.0 %copy-start.9 = (bf16[1,32,4,8,256]{4,1,3,2,0:T(8,128)(2,1)S(1)}, bf16[1,32,4,8,256]{4,1,3,2,0:T(8,128)(2,1)}, u32[]{:S(2)}) copy-start(bf16[1,32,4,8,256]{4,1,3,2,0:T(8,128)(2,1)} %get-tuple-element.47) | copy-start | bytes 1572868
  66.5 11.0 %copy-start.2 = (bf16[32,4,8,256]{3,2,1,0:T(8,128)(2,1)S(1)}, bf16[32,4,8,256]{3,2,1,0:T(8,128)(2,1)}, u32[]{:S(2)}) copy-start(bf16[32,4,8,256]{3,2,1,0:T(8,128)(2,1)} %param.6) | copy-start | bytes 1572868
  71.9 9.0 %copy-start.18 = (bf16[1,32,4,8,256]{4,1,3,2,0:T(8,128)(2,1)S(1)}, bf16[1,32,4,8,256]{4,1,3,2,0:T(8,128)(2,1)}, u32[]{:S(2)}) copy-start(bf16[1,32,4,8,256]{4,1,3,2,0:T(8,128)(2,1)} %get-tuple-element.39) | copy-start | bytes 1572868
  71.9 9.0 %copy-start.19 = (bf16[1,32,4,8,256]{4,1,3,2,0:T(8,128)(2,1)S(1)}, bf16[1,32,4,8,256]{4,1,3,2,0:T(8,128)(2,1)}, u32[]{:S(2)}) copy-start(bf16[1,32,4,8,256]{4,1,3,2,0:T(8,128)(2,1)} %get-tuple-element.45) | copy-start | bytes 1572868
  74.1 8.4 %copy-start.23 = (bf16[1,32,4,8,256]{4,1,3,2,0:T(8,128)(2,1)S(1)}, bf16[1,32,4,8,256]{4,1,3,2,0:T(8,128)(2,1)}, u32[]{:S(2)}) copy-start(bf16[1,32,4,8,256]{4,1,3,2,0:T(8,128)(2,1)} %get-tuple-element.54) | copy-start | bytes 1572868
  84.6 10.5 %copy-start.5 = (bf16[1,32,4,8,256]{4,1,3,2,0:T(8,128)(2,1)S(1)}, bf16[1,32,4,8,256]{4,1,3,2,0:T(8,128)(2,1)}, u32[]{:S(2)}) copy-start(bf16[1,32,4,8,256]{4,1,3,2,0:T(8,128)(2,1)} %get-tuple-element.36) | copy-start | bytes 1572868
  96.2 11.0 %copy-start.20 = (bf16[1,32,4,8,256]{4,1,3,2,0:T(8,128)(2,1)S(1)}, bf16[1,32,4,8,256]{4,1,3,2,0:T(8,128)(2,1)}, u32[]{:S(2)}) copy-start(bf16[1,32,4,8,256]{4,1,3,2,0:T(8,128)(2,1)} %get-tuple-element.55) | copy-start | bytes 1572868
  117.7 6.9 %slice-start.2 = ((s8[4718592]{0:T(1024)(128)(4,1)}), s8[4194304]{0:T(1024)(128)(4,1)S(1)}, s32[]{:S(2)}) async-start(s8[4718592]{0:T(1024)(128)(4,1)} %bitcast.233), calls=%async_computation.2 | async-start | bytes 8388608
  125.8 7.2 %collective-permute-start.6 = (bf16[32,1,8,256]{3,2,1,0:T(8,128)(2,1)S(1)}, bf16[32,1,8,256]{3,2,1,0:T(8,128)(2,1)S(1)}, u32[]{:S(2)}, u32[]{:S(2)}) collective-permute-start(bf16[32,1,8,256]{3,2,1,0:T(8,128)(2,1)S(1)} %get-tuple-element.69), channel_id=1, source_target_pairs={{0,4},{4,8},{8,12},{1,5},{5,9},{9,13},{2,6},{6,10},{10,14},{3,7},{... | collective-permute-start | bytes 393224 | tf_op jit(solution)/shard_map/ppermute | solution.py:16
  129.8 8.1 %collective-permute-start.7 = (bf16[32,1,8,256]{3,2,1,0:T(8,128)(2,1)S(1)}, bf16[32,1,8,256]{3,2,1,0:T(8,128)(2,1)S(1)}, u32[]{:S(2)}, u32[]{:S(2)}) collective-permute-start(bf16[32,1,8,256]{3,2,1,0:T(8,128)(2,1)S(1)} %get-tuple-element.68), channel_id=1, source_target_pairs={{4,0},{8,4},{12,8},{5,1},{9,5},{13,9},{6,2},{10,6},{14,10},{7,3},{... | collective-permute-start | bytes 393224 | tf_op jit(solution)/shard_map/ppermute | solution.py:17
  138.0 26.0 %copy-start.28 = (bf16[32,1,8,256]{3,2,1,0:T(8,128)(2,1)}, bf16[32,1,8,256]{3,2,1,0:T(8,128)(2,1)S(1)}, u32[]{:S(2)}) copy-start(bf16[32,1,8,256]{3,2,1,0:T(8,128)(2,1)S(1)} %collective-permute-done.7) | copy-start | bytes 393220
  142.9 12.9 %collective-permute-start.8 = (bf16[32,6,1,256]{0,1,3,2:T(8,128)(2,1)S(1)}, bf16[32,6,1,256]{0,1,3,2:T(8,128)(2,1)S(1)}, u32[]{:S(2)}, u32[]{:S(2)}) collective-permute-start(bf16[32,6,1,256]{0,1,3,2:T(8,128)(2,1)S(1)} %get-tuple-element.8), channel_id=1, source_target_pairs={{0,2},{1,3},{4,6},{5,7},{8,10},{9,11},{12,14},{13,15},{16,18},{17,... | collective-permute-start | bytes 294920 | tf_op jit(solution)/shard_map/ppermute | solution.py:16
  144.5 15.4 %collective-permute-start.9 = (bf16[32,6,1,256]{0,1,3,2:T(8,128)(2,1)S(1)}, bf16[32,6,1,256]{0,1,3,2:T(8,128)(2,1)S(1)}, u32[]{:S(2)}, u32[]{:S(2)}) collective-permute-start(bf16[32,6,1,256]{0,1,3,2:T(8,128)(2,1)S(1)} %get-tuple-element.9), channel_id=1, source_target_pairs={{2,0},{3,1},{6,4},{7,5},{10,8},{11,9},{14,12},{15,13},{18,16},{19,... | collective-permute-start | bytes 294920 | tf_op jit(solution)/shard_map/ppermute | solution.py:17
  159.9 4.1 %copy-start.16 = (bf16[32,6,1,256]{0,1,3,2:T(8,128)(2,1)}, bf16[32,6,1,256]{0,1,3,2:T(8,128)(2,1)S(1)}, u32[]{:S(2)}) copy-start(bf16[32,6,1,256]{0,1,3,2:T(8,128)(2,1)S(1)} %collective-permute-done.9) | copy-start | bytes 294916
  167.0 11.2 %collective-permute-start.10 = (bf16[32,6,10,1]{0,1,3,2:T(8,128)(2,1)}, bf16[32,6,10,1]{0,1,3,2:T(8,128)(2,1)}, u32[]{:S(2)}, u32[]{:S(2)}) collective-permute-start(bf16[32,6,10,1]{0,1,3,2:T(8,128)(2,1)} %get-tuple-element.5), channel_id=1, source_target_pairs={{0,1},{2,3},{4,5},{6,7},{8,9},{10,11},{12,13},{14,15},{16,17},{18,... | collective-permute-start | bytes 11528 | tf_op jit(solution)/shard_map/ppermute | solution.py:16
  168.8 15.3 %collective-permute-start.11 = (bf16[32,6,10,1]{0,1,3,2:T(8,128)(2,1)}, bf16[32,6,10,1]{0,1,3,2:T(8,128)(2,1)}, u32[]{:S(2)}, u32[]{:S(2)}) collective-permute-start(bf16[32,6,10,1]{0,1,3,2:T(8,128)(2,1)} %get-tuple-element.4), channel_id=1, source_target_pairs={{1,0},{3,2},{5,4},{7,6},{9,8},{11,10},{13,12},{15,14},{17,16},{19,... | collective-permute-start | bytes 11528 | tf_op jit(solution)/shard_map/ppermute | solution.py:17
  186.1 5.5 %copy-start.15 = (bf16[1,32,4,8,256]{4,1,3,2,0:T(8,128)(2,1)S(1)}, bf16[1,32,4,8,256]{4,1,3,2,0:T(8,128)(2,1)}, u32[]{:S(2)}) copy-start(bf16[1,32,4,8,256]{4,1,3,2,0:T(8,128)(2,1)} %get-tuple-element.28) | copy-start | bytes 1572868
  186.1 9.8 %copy-start.13 = (bf16[1,32,4,8,256]{4,1,3,2,0:T(8,128)(2,1)S(1)}, bf16[1,32,4,8,256]{4,1,3,2,0:T(8,128)(2,1)}, u32[]{:S(2)}) copy-start(bf16[1,32,4,8,256]{4,1,3,2,0:T(8,128)(2,1)} %get-tuple-element.23) | copy-start | bytes 1572868
  186.1 10.9 %copy-start.27 = (bf16[1,32,4,8,256]{4,1,3,2,0:T(8,128)(2,1)S(1)}, bf16[1,32,4,8,256]{4,1,3,2,0:T(8,128)(2,1)}, u32[]{:S(2)}) copy-start(bf16[1,32,4,8,256]{4,1,3,2,0:T(8,128)(2,1)} %get-tuple-element.62) | copy-start | bytes 1572868
  186.1 13.1 %copy-start.11 = (bf16[1,32,4,8,256]{4,1,3,2,0:T(8,128)(2,1)S(1)}, bf16[1,32,4,8,256]{4,1,3,2,0:T(8,128)(2,1)}, u32[]{:S(2)}) copy-start(bf16[1,32,4,8,256]{4,1,3,2,0:T(8,128)(2,1)} %get-tuple-element.29) | copy-start | bytes 1572868
  191.6 8.8 %copy-start.29 = (bf16[32,1,8,256]{3,2,1,0:T(8,128)(2,1)S(1)}, bf16[32,1,8,256]{3,2,1,0:T(8,128)(2,1)}, u32[]{:S(2)}) copy-start(bf16[32,1,8,256]{3,2,1,0:T(8,128)(2,1)} %copy-done.28) | copy-start | bytes 393220
  192.7 9.9 %copy-start.8 = (bf16[1,32,4,8,256]{4,1,3,2,0:T(8,128)(2,1)S(1)}, bf16[1,32,4,8,256]{4,1,3,2,0:T(8,128)(2,1)}, u32[]{:S(2)}) copy-start(bf16[1,32,4,8,256]{4,1,3,2,0:T(8,128)(2,1)} %get-tuple-element.21) | copy-start | bytes 1572868
  194.9 8.8 %copy-start.24 = (bf16[1,32,4,8,256]{4,1,3,2,0:T(8,128)(2,1)S(1)}, bf16[1,32,4,8,256]{4,1,3,2,0:T(8,128)(2,1)}, u32[]{:S(2)}) copy-start(bf16[1,32,4,8,256]{4,1,3,2,0:T(8,128)(2,1)} %get-tuple-element.48) | copy-start | bytes 1572868
  214.2 9.6 %copy-start.7 = (bf16[1,32,4,8,256]{4,1,3,2,0:T(8,128)(2,1)S(1)}, bf16[1,32,4,8,256]{4,1,3,2,0:T(8,128)(2,1)}, u32[]{:S(2)}) copy-start(bf16[1,32,4,8,256]{4,1,3,2,0:T(8,128)(2,1)} %get-tuple-element.17) | copy-start | bytes 1572868
  214.2 10.6 %copy-start.3 = (bf16[1,32,4,8,256]{4,1,3,2,0:T(8,128)(2,1)S(1)}, bf16[1,32,4,8,256]{4,1,3,2,0:T(8,128)(2,1)}, u32[]{:S(2)}) copy-start(bf16[1,32,4,8,256]{4,1,3,2,0:T(8,128)(2,1)} %get-tuple-element.27) | copy-start | bytes 1572868
  214.2 11.7 %copy-start.22 = (bf16[1,32,4,8,256]{4,1,3,2,0:T(8,128)(2,1)S(1)}, bf16[1,32,4,8,256]{4,1,3,2,0:T(8,128)(2,1)}, u32[]{:S(2)}) copy-start(bf16[1,32,4,8,256]{4,1,3,2,0:T(8,128)(2,1)} %get-tuple-element.50) | copy-start | bytes 1572868
  214.2 12.8 %copy-start.6 = (bf16[1,32,4,8,256]{4,1,3,2,0:T(8,128)(2,1)S(1)}, bf16[1,32,4,8,256]{4,1,3,2,0:T(8,128)(2,1)}, u32[]{:S(2)}) copy-start(bf16[1,32,4,8,256]{4,1,3,2,0:T(8,128)(2,1)} %get-tuple-element.18) | copy-start | bytes 1572868
  228.1 8.6 %copy-start.4 = (bf16[1,32,4,8,256]{4,1,3,2,0:T(8,128)(2,1)S(1)}, bf16[1,32,4,8,256]{4,1,3,2,0:T(8,128)(2,1)}, u32[]{:S(2)}) copy-start(bf16[1,32,4,8,256]{4,1,3,2,0:T(8,128)(2,1)} %get-tuple-element.14) | copy-start | bytes 1572868
  228.1 10.8 %copy-start.21 = (bf16[1,32,4,8,256]{4,1,3,2,0:T(8,128)(2,1)S(1)}, bf16[1,32,4,8,256]{4,1,3,2,0:T(8,128)(2,1)}, u32[]{:S(2)}) copy-start(bf16[1,32,4,8,256]{4,1,3,2,0:T(8,128)(2,1)} %get-tuple-element.49) | copy-start | bytes 1572868
  249.3 6.9 %slice-start = ((s8[4718592]{0:T(1024)(128)(4,1)}), s8[4194304]{0:T(1024)(128)(4,1)S(1)}, s32[]{:S(2)}) async-start(s8[4718592]{0:T(1024)(128)(4,1)} %bitcast.231), calls=%async_computation | async-start | bytes 8388608
  257.3 9.0 %copy-start.30 = (s32[4,1,1,256]{3,2,1,0:T(1,128)S(1)}, s32[4,1,1,256]{3,2,1,0:T(1,128)}, u32[]{:S(2)}) copy-start(s32[4,1,1,256]{3,2,1,0:T(1,128)} %param.10) | copy-start | bytes 12292
  257.3 9.0 %copy-start.32 = (s32[4,4]{1,0:T(4,128)S(1)}, s32[4,4]{1,0:T(4,128)}, u32[]{:S(2)}) copy-start(s32[4,4]{1,0:T(4,128)} %param.11) | copy-start | bytes 196
  257.8 23.1 %copy-start.17 = (bf16[32,4,8,256]{3,2,1,0:T(8,128)(2,1)}, bf16[32,4,8,256]{3,2,1,0:T(8,128)(2,1)S(1)}, u32[]{:S(2)}) copy-start(bf16[32,4,8,256]{3,2,1,0:T(8,128)(2,1)S(1)} %add_convert_fusion) | copy-start | bytes 1572868
  260.2 6.1 %collective-permute-start.12 = (bf16[1,32,256]{1,2,0:T(8,128)(2,1)S(1)}, bf16[1,32,256]{1,2,0:T(8,128)(2,1)S(1)}, u32[]{:S(2)}, u32[]{:S(2)}) collective-permute-start(bf16[1,32,256]{1,2,0:T(8,128)(2,1)S(1)} %divide_convert_fusion), channel_id=1, source_target_pairs={{0,4},{4,8},{8,12},{12,0},{1,5},{5,9},{9,13},{13,1},{2,6},{6,10},{... | collective-permute-start | bytes 49160 | tf_op jit(solution)/shard_map/ppermute | solution.py:60
  266.3 6.4 %collective-permute-start.13 = (bf16[1,32,256]{1,2,0:T(8,128)(2,1)S(1)}, bf16[1,32,256]{1,2,0:T(8,128)(2,1)S(1)}, u32[]{:S(2)}, u32[]{:S(2)}) collective-permute-start(bf16[1,32,256]{1,2,0:T(8,128)(2,1)S(1)} %collective-permute-done.12), channel_id=1, source_target_pairs={{0,4},{4,8},{8,12},{12,0},{1,5},{5,9},{9,13},{13,1},{2,6},{6,10},{... | collective-permute-start | bytes 49160 | tf_op jit(solution)/shard_map/ppermute | solution.py:60
  272.6 6.1 %collective-permute-start.14 = (bf16[1,32,256]{1,2,0:T(8,128)(2,1)S(1)}, bf16[1,32,256]{1,2,0:T(8,128)(2,1)S(1)}, u32[]{:S(2)}, u32[]{:S(2)}) collective-permute-start(bf16[1,32,256]{1,2,0:T(8,128)(2,1)S(1)} %collective-permute-done.13), channel_id=1, source_target_pairs={{0,4},{4,8},{8,12},{12,0},{1,5},{5,9},{9,13},{13,1},{2,6},{6,10},{... | collective-permute-start | bytes 49160 | tf_op jit(solution)/shard_map/ppermute | solution.py:60
  (5 other events, 14.2 us)
